TPU v7x, 256 devices: a whole 4x4x8 slice. The times are simulated.
256 devices in a mesh: aux: 2 (over core), row: 8 (over z), col: 16 (over x, y).
Axes of the slice: x: 4, y: 4, z: 8, core: 2. Of those that a mesh axis runs over, the one named last changes fastest.
Arguments:
- coulomb: bfloat16 [64, 2048, 2048], P('aux', 'row', 'col'), may hold values from -6 to 6
- occupied: bfloat16 [2048, 2048], P('row'), may hold values from -0.125 to 0.125
- virtual: bfloat16 [2048, 2048], P('row'), may hold values from -0.125 to 0.125
- tile_mask: int32 [16, 16], replicated, may hold values 0 or 1
Outputs:
- chi: float32 [64, 64], P('aux')
All inputs are finite; a program needn't handle non-finite values.
Results may differ from a plain program's by a relative error of at most 0.0042.
Values may be sent and summed in bfloat16 or wider, within the bound.
A program may use at most 128 MiB of HBM per device.

v0:
```python
import jax
import jax.numpy as jnp
from jax import lax
from jax.sharding import PartitionSpec as P

NAO = 2048
TILE = 128


def swapped(value, axis, apart):
    mask = 2**apart
    pairs = [(source, source ^ mask) for source in range(lax.axis_size(axis))]
    return lax.ppermute(value, axis, pairs)


def shards(coulomb, occupied, virtual, tile_mask):
    rows = lax.axis_size("row")
    cols = lax.axis_size("col")
    pdev, mrow, ncol = coulomb.shape
    nao = mrow * rows
    row_idx = lax.axis_index("row")
    col_idx = lax.axis_index("col")
    aux_idx = lax.axis_index("aux")
    tiles_r = mrow // TILE
    tiles_c = ncol // TILE
    local_tiles = lax.dynamic_slice(
        tile_mask, (row_idx * tiles_r, col_idx * tiles_c), (tiles_r, tiles_c)
    )
    local_mask = jnp.repeat(jnp.repeat(local_tiles, TILE, axis=0), TILE, axis=1).astype(
        jnp.bfloat16
    )
    screened = coulomb * local_mask[None]
    moved = lax.all_to_all(screened, "row", split_axis=0, concat_axis=1, tiled=True)
    pieces = moved.shape[0]
    occ_all, virt_all = (
        lax.all_gather(occupied, "row", axis=0, tiled=True),
        lax.all_gather(virtual, "row", axis=0, tiled=True),
    )
    half = jnp.einsum("ml,pmn->pln", occ_all, moved, preferred_element_type=jnp.float32).astype(
        jnp.bfloat16
    )
    jpart = mrow // cols
    shaped = half.reshape(pieces, rows, cols, jpart, ncol)
    spread = lax.all_to_all(shaped, "col", split_axis=2, concat_axis=4, tiled=True)
    spread = spread.reshape(pieces, rows * jpart, nao)
    dressed = jnp.einsum(
        "pln,ns->pls", spread, virt_all, preferred_element_type=jnp.float32
    ).astype(jnp.bfloat16)
    layered = dressed.reshape(pieces, rows, 1, jpart, cols, ncol)
    returned = lax.all_to_all(
        lax.all_to_all(layered, "row", split_axis=1, concat_axis=0, tiled=True),
        "col",
        split_axis=4,
        concat_axis=2,
        tiled=True,
    )
    aligned = returned.reshape(pdev, mrow, ncol)
    theirs = swapped(screened, "aux", 0)
    with_mine = jnp.einsum("pls,qls->pq", aligned, screened, preferred_element_type=jnp.float32)
    with_theirs = jnp.einsum("pls,qls->pq", aligned, theirs, preferred_element_type=jnp.float32)
    first_half = jnp.where(aux_idx == 0, with_mine, with_theirs)
    second_half = jnp.where(aux_idx == 0, with_theirs, with_mine)
    partial_chi = jnp.concatenate([first_half, second_half], axis=1)
    slots = lax.axis_size("aux")
    placed = jnp.zeros((slots,) + partial_chi.shape, partial_chi.dtype)
    placed = lax.dynamic_update_index_in_dim(placed, partial_chi, aux_idx, 0)
    total = lax.psum(placed, ("aux", "row", "col"))
    total_chi = lax.dynamic_index_in_dim(total, aux_idx, 0, keepdims=False)
    return total_chi / NAO


def solution(mesh):
    placed = (P("aux", "row", "col"), P("row", None), P("row", None), P())
    return jax.shard_map(
        shards, mesh=mesh, in_specs=placed, out_specs=P("aux", None), check_vma=False
    )
```

profile of v0, /device:TPU:1, one launch (start us, length us, event | category | flops | bytes accessed | tf_op | source)
XLA Modules:
  0.0 430.4 jit_solution(17136864265026919637)
XLA Ops:
  6.5 0.0 all-gather.3.cloned.1.call-start
  6.5 0.7 all-gather.3.cloned.1.call-update
  7.3 0.0 all-gather.5.cloned.1.call-start
  7.3 0.7 all-gather.5.cloned.1.call-update
  8.0 0.9 fusion.14
  8.9 0.1 broadcast_bitcast_fusion
  9.0 2.8 copy_multiply_fusion
  11.7 0.8 copy.15
  12.6 79.7 %all_to_all.66 = bf16[32,256,128]{2,1,0:T(8,128)(2,1)} all-to-all(bf16[32,256,128]{2,1,0:T(8,128)(2,1)S(1)} %copy.15), channel_id=1, replica_groups=mesh['aux'=2,'row'=8,'col'=16] {'row'}, dimensions={0} | all-to-all | bytes 4194304 | tf_op jit(solution)/shard_map/all_to_all | solution.py:33
  92.2 4.5 %copy.16 = bf16[8,4,256,128]{2,0,3,1:T(8,128)(2,1)} copy(bf16[8,4,256,128]{3,2,1,0:T(8,128)(2,1)} %bitcast.62) | data formatting | bytes 4194304 | tf_op jit(solution)/shard_map/all_to_all | solution.py:33
  96.7 4.2 all_to_all.51
  100.9 48.7 %all-gather.3.cloned.1.call-done = bf16[2048,2048]{1,0:T(8,128)(2,1)} async-done(((bf16[256,2048]{1,0:T(8,128)(2,1)}), bf16[2048,2048]{1,0:T(8,128)(2,1)}) %all-gather.3.cloned.1.call-update) | async-done | bytes 8388624 | tf_op jit(solution)/shard_map/all_gather | solution.py:36
  149.7 9.8 %fusion.10 = bf16[4,2048,128]{1,2,0:T(8,128)(2,1)} fusion(bf16[4,2048,128]{1,2,0:T(8,128)(2,1)} %all_to_all.51, bf16[2048,2048]{1,0:T(8,128)(2,1)} %all-gather.3.cloned.1.call-done), kind=kOutput, calls=%fused_computation.6 | convolution fusion | flops 4296015872 | bytes 12582912 | tf_op jit(solution)/shard_map/ml,pmn->pln/dot_general | solution.py:39
  159.5 4.0 copy.17
  163.4 2.2 copy.18
  165.6 33.7 %all_to_all.67 = bf16[4,8,16,16,128]{4,3,1,0,2:T(8,128)(2,1)S(1)} all-to-all(bf16[4,8,16,16,128]{4,3,1,0,2:T(8,128)(2,1)S(1)} %copy.18), channel_id=1, replica_groups=mesh['aux'=2,'row'=8,'col'=16] {'col'}, dimensions={2} | all-to-all | bytes 4194304 | tf_op jit(solution)/shard_map/all_to_all | solution.py:44
  199.3 3.7 copy.19
  203.1 4.2 reshape.37
  207.3 37.2 %all-gather.5.cloned.1.call-done = bf16[2048,2048]{1,0:T(8,128)(2,1)} async-done(((bf16[256,2048]{1,0:T(8,128)(2,1)}), bf16[2048,2048]{1,0:T(8,128)(2,1)}) %all-gather.5.cloned.1.call-update) | async-done | bytes 8388624 | tf_op jit(solution)/shard_map/all_gather | solution.py:37
  244.4 8.5 %fusion.7 = bf16[4,128,2048]{2,1,0:T(8,128)(2,1)S(1)} fusion(bf16[4,128,2048]{2,1,0:T(8,128)(2,1)} %reshape.37, bf16[2048,2048]{1,0:T(8,128)(2,1)} %all-gather.5.cloned.1.call-done), kind=kOutput, calls=%fused_computation.5 | convolution fusion | flops 4296015872 | bytes 12582912 | tf_op jit(solution)/shard_map/pln,ns->pls/dot_general | solution.py:46
  253.0 0.6 copy.23
  253.6 0.6 copy.20
  254.2 53.5 %all_to_all.68 = bf16[4,8,1,16,16,128]{5,4,3,0,2,1:T(8,128)(2,1)S(1)} all-to-all(bf16[4,8,1,16,16,128]{5,4,3,0,2,1:T(8,128)(2,1)S(1)} %copy.20), channel_id=1, replica_groups=mesh['aux'=2,'row'=8,'col'=16] {'row'}, dimensions={1} | all-to-all | bytes 4194304 | tf_op jit(solution)/shard_map/all_to_all | solution.py:51
  307.7 1.8 copy.21
  309.6 6.6 %all-to-all-start.3 = ((bf16[32,1,1,16,16,128]{5,3,0,2,1,4:T(8,128)(2,1)}), bf16[32,1,1,16,16,128]{5,3,0,2,1,4:T(8,128)(2,1)}, u32[]{:S(2)}, u32[]{:S(2)}) async-start(bf16[32,1,1,16,16,128]{5,3,0,2,1,4:T(8,128)(2,1)} %copy.21), calls=%async_computation.3 | async-start | bytes 4194304 | tf_op jit(solution)/shard_map/all_to_all | solution.py:50
  316.2 2.8 collective-permute-start
  319.0 22.5 %all-to-all-done.3 = bf16[32,1,1,16,16,128]{5,3,0,2,1,4:T(8,128)(2,1)} async-done(((bf16[32,1,1,16,16,128]{5,3,0,2,1,4:T(8,128)(2,1)}), bf16[32,1,1,16,16,128]{5,3,0,2,1,4:T(8,128)(2,1)}, u32[]{:S(2)}, u32[]{:S(2)}) %all-to-all-start.3) | async-done | bytes 2097184 | tf_op jit(solution)/shard_map/all_to_all | solution.py:50
  341.5 2.1 copy.22
  343.6 0.7 convolution_bitcast_fusion.1
  344.3 0.0 collective-permute-done
  344.3 2.3 broadcast_select_fusion.1
  346.6 0.1 fusion.13
  346.7 76.2 %psum.7 = f32[2,32,64]{2,1,0:T(8,128)S(1)} all-reduce(f32[2,32,64]{2,1,0:T(8,128)S(1)} %fusion.13), channel_id=1, replica_groups=mesh['aux'=2,'row'=8,'col'=16] {'aux','row','col'}, use_global_device_ids=true, to_apply=%region_0.1 | all-reduce | flops 4096 | bytes 32768 | tf_op jit(solution)/shard_map/psum | solution.py:67
  422.9 0.6 multiply_bitcast_fusion
  (1 shorter events, 0.0 us)
Async XLA Ops:
  6.5 143.1 %all-gather.3.cloned.1.call-start = ((), (), s32[]{:S(2)}) async-start(), calls=%async_computation.4 | async-start | bytes 9437184 | tf_op jit(solution)/shard_map/all_gather | solution.py:36
  7.3 237.2 %all-gather.5.cloned.1.call-start = ((), (), s32[]{:S(2)}) async-start(), calls=%async_computation.5 | async-start | bytes 9437184 | tf_op jit(solution)/shard_map/all_gather | solution.py:37
  309.6 31.9 %all-to-all-start.3 = ((bf16[32,1,1,16,16,128]{5,3,0,2,1,4:T(8,128)(2,1)}), bf16[32,1,1,16,16,128]{5,3,0,2,1,4:T(8,128)(2,1)}, u32[]{:S(2)}, u32[]{:S(2)}) async-start(bf16[32,1,1,16,16,128]{5,3,0,2,1,4:T(8,128)(2,1)} %copy.21), calls=%async_computation.3 | async-start | bytes 4194304 | tf_op jit(solution)/shard_map/all_to_all | solution.py:50
  316.2 28.2 %collective-permute-start = (bf16[32,256,128]{2,0,1:T(8,128)(2,1)S(1)}, bf16[32,256,128]{2,0,1:T(8,128)(2,1)}, u32[]{:S(2)}, u32[]{:S(2)}) collective-permute-start(bf16[32,256,128]{2,0,1:T(8,128)(2,1)S(1)} %copy_multiply_fusion), channel_id=1, source_target_pairs={{0,128},{128,0},{1,129},{129,1},{2,130},{130,2},{3,131},{131,3},{4... | collective-permute-start | bytes 6291464 | tf_op jit(solution)/shard_map/ppermute | solution.py:13
Sparse Core Ops, SparseCore 0:
  9.1 140.4 all-gather.2
  151.4 92.9 all-gather.4
where the time goes:
time: 431 us; the launch traced here: 430 us
  blocking collectives  243 us (56%)
  waiting for transfers between devices  110 us (26%)
  local copies, waits for them, and re-layouts  28.9 us (7%)
  matrix products  21.3 us (5%)
  between operations  13.5 us (3%)
  starting transfers between devices  9.44 us (2%)
  other arithmetic  4.33 us (1%)
    all_to_all x1, blocking collectives, shards(): lax.all_to_all(screened, 'row', split_axis=0, concat_axis=1, tiled=True)  79.7 us
    psum x1, blocking collectives, shards(): total = lax.psum(placed, ('aux', 'row', 'col'))  76.2 us
    all_to_all x1, blocking collectives, shards(): lax.all_to_all(layered, 'row', split_axis=1, concat_axis=0, tiled=True)  53.5 us
    all_gather x1, waiting for transfers between devices, shards(): lax.all_gather(occupied, 'row', axis=0, tiled=True)  48.7 us
    all_gather x1, waiting for transfers between devices, shards(): lax.all_gather(virtual, 'row', axis=0, tiled=True)  37.2 us
    all_to_all x1, blocking collectives, shards(): lax.all_to_all(shaped, 'col', split_axis=2, concat_axis=4, tiled=True)  33.7 us
    all_to_all x1, waiting for transfers between devices, shards(): lax.all_to_all(lax.all_to_all(layered, 'row', split_axis=1, concat_axis=0...  22.5 us
    dot_general x1, matrix products, shards(): jnp.einsum('ml,pmn->pln', occ_all, moved, preferred_element_type=jnp.floa...  9.81 us
  transfers between devices with their start and end apart: 4, of which 3 were waited for; matrix products, arithmetic and copies ran while one was open for 8% of the time, Pallas kernels for 0%

commit v1 on v0

--- a/solution.py
+++ b/solution.py
@@ -33,7 +33,9 @@
     moved = lax.all_to_all(screened, "row", split_axis=0, concat_axis=1, tiled=True)
     pieces = moved.shape[0]
     occ_all, virt_all = (
-        lax.all_gather(occupied, "row", axis=0, tiled=True),
+        jnp.concatenate(
+            lax.all_to_all(jnp.stack([occupied] * lax.axis_size("row")), "row", 0, 0), axis=0
+        ),
         lax.all_gather(virtual, "row", axis=0, tiled=True),
     )
     half = jnp.einsum("ml,pmn->pln", occ_all, moved, preferred_element_type=jnp.float32).astype(

time: 431 us -> 585 us (1.36)
  waiting for transfers between devices: 110 us -> 282 us
  blocking collectives: 243 us -> 221 us
    all_to_all x0 -> x1, waiting for transfers between devices: none -> 261 us  [shards(): lax.all_to_all(jnp.stack([occupied] * lax.axis_size('row')), 'row', 0, 0)]
    all_gather x1 -> x0, waiting for transfers between devices: 48.7 us -> none  [shards(): lax.all_gather(occupied, 'row', axis=0, tiled=True)]
    all_gather x1, waiting for transfers between devices: 37.2 us -> 0.01 us  [shards(): lax.all_gather(virtual, 'row', axis=0, tiled=True)]
    all_to_all x1, blocking collectives: 79.7 us -> 58.7 us  [shards(): lax.all_to_all(screened, 'row', split_axis=0, concat_axis=1, tiled=True)]
  transfers between devices with their start and end apart: 4 -> 4, of which waited for: 3 -> 2; matrix products, arithmetic and copies ran while one was open for 8% -> 5% of each run, Pallas kernels for 0% -> 0%
where the time goes in v1:
time: 585 us; the launch traced here: 584 us
  waiting for transfers between devices  282 us (48%)
  blocking collectives  221 us (38%)
  local copies, waits for them, and re-layouts  28.3 us (5%)
  matrix products  21.3 us (4%)
  starting transfers between devices  13.5 us (2%)
  between operations  13.5 us (2%)
    all_to_all x1, waiting for transfers between devices, shards(): lax.all_to_all(jnp.stack([occupied] * lax.axis_size('row')), 'row', 0, 0)  261 us
    psum x1, blocking collectives, shards(): total = lax.psum(placed, ('aux', 'row', 'col'))  77.7 us
    all_to_all x1, blocking collectives, shards(): lax.all_to_all(screened, 'row', split_axis=0, concat_axis=1, tiled=True)  58.7 us
    all_to_all x1, blocking collectives, shards(): lax.all_to_all(layered, 'row', split_axis=1, concat_axis=0, tiled=True)  50.7 us
    all_to_all x1, blocking collectives, shards(): lax.all_to_all(shaped, 'col', split_axis=2, concat_axis=4, tiled=True)  33.7 us
    all_to_all x1, waiting for transfers between devices, shards(): lax.all_to_all(lax.all_to_all(layered, 'row', split_axis=1, concat_axis=0...  21.2 us
  transfers between devices with their start and end apart: 4, of which 2 were waited for; matrix products, arithmetic and copies ran while one was open for 5% of the time, Pallas kernels for 0%

profile of v1, /device:TPU:1, one launch (start us, length us, event | category | flops | bytes accessed | tf_op | source)
XLA Modules:
  0.0 584.2 jit_solution(5476880884890782233)
XLA Ops:
  6.5 0.9 fusion.14
  7.4 0.1 broadcast_bitcast_fusion
  7.5 2.8 copy_multiply_fusion
  10.3 0.8 copy.15
  11.1 0.0 copy-start
  11.1 58.7 %all_to_all.68 = bf16[32,256,128]{2,1,0:T(8,128)(2,1)} all-to-all(bf16[32,256,128]{2,1,0:T(8,128)(2,1)S(1)} %copy.15), channel_id=1, replica_groups=mesh['aux'=2,'row'=8,'col'=16] {'row'}, dimensions={0} | all-to-all | bytes 4194304 | tf_op jit(solution)/shard_map/all_to_all | solution.py:33
  69.8 0.0 copy-done
  69.8 4.3 stack.2
  74.1 5.0 all-to-all-start.1
  79.1 0.0 all-gather.2.cloned.1.call-start
  79.2 0.7 all-gather.2.cloned.1.call-update
  79.9 3.9 copy.16
  83.8 260.5 %all-to-all-done.1 = bf16[8,256,2048]{2,1,0:T(8,128)(2,1)} async-done(((bf16[8,256,2048]{2,1,0:T(8,128)(2,1)}), bf16[8,256,2048]{2,1,0:T(8,128)(2,1)}, u32[]{:S(2)}, u32[]{:S(2)}) %all-to-all-start.1) | async-done | bytes 8388640 | tf_op jit(solution)/shard_map/all_to_all | solution.py:37
  344.3 9.8 %fusion.9 = bf16[4,2048,128]{1,2,0:T(8,128)(2,1)} fusion(bf16[8,256,2048]{2,1,0:T(8,128)(2,1)} %all-to-all-done.1, bf16[8,4,256,128]{2,3,1,0:T(8,128)(2,1)} %copy.16), kind=kOutput, calls=%fused_computation.6 | convolution fusion | flops 4296015872 | bytes 12582912 | tf_op jit(solution)/shard_map/ml,pmn->pln/dot_general | solution.py:41
  354.1 3.9 copy.17
  358.1 2.2 copy.18
  360.3 33.7 %all_to_all.69 = bf16[4,8,16,16,128]{4,3,1,0,2:T(8,128)(2,1)S(1)} all-to-all(bf16[4,8,16,16,128]{4,3,1,0,2:T(8,128)(2,1)S(1)} %copy.18), channel_id=1, replica_groups=mesh['aux'=2,'row'=8,'col'=16] {'col'}, dimensions={2} | all-to-all | bytes 4194304 | tf_op jit(solution)/shard_map/all_to_all | solution.py:46
  394.0 3.7 copy.19
  397.7 4.2 reshape.40
  401.9 0.0 all-gather.2.cloned.1.call-done
  401.9 8.5 %fusion.6 = bf16[4,128,2048]{2,1,0:T(8,128)(2,1)S(1)} fusion(bf16[4,128,2048]{2,1,0:T(8,128)(2,1)} %reshape.40, bf16[2048,2048]{1,0:T(8,128)(2,1)} %all-gather.2.cloned.1.call-done), kind=kOutput, calls=%fused_computation.5 | convolution fusion | flops 4296015872 | bytes 12582912 | tf_op jit(solution)/shard_map/pln,ns->pls/dot_general | solution.py:48
  410.5 0.6 copy.24
  411.1 0.6 copy.20
  411.7 50.7 %all_to_all.70 = bf16[4,8,1,16,16,128]{5,4,3,0,2,1:T(8,128)(2,1)S(1)} all-to-all(bf16[4,8,1,16,16,128]{5,4,3,0,2,1:T(8,128)(2,1)S(1)} %copy.20), channel_id=1, replica_groups=mesh['aux'=2,'row'=8,'col'=16] {'row'}, dimensions={1} | all-to-all | bytes 4194304 | tf_op jit(solution)/shard_map/all_to_all | solution.py:53
  462.4 1.8 copy.21
  464.2 4.5 all-to-all-start.4
  468.8 3.9 collective-permute-start
  472.7 21.2 %all-to-all-done.4 = bf16[32,1,1,16,16,128]{5,3,0,2,1,4:T(8,128)(2,1)} async-done(((bf16[32,1,1,16,16,128]{5,3,0,2,1,4:T(8,128)(2,1)}), bf16[32,1,1,16,16,128]{5,3,0,2,1,4:T(8,128)(2,1)}, u32[]{:S(2)}, u32[]{:S(2)}) %all-to-all-start.4) | async-done | bytes 2097184 | tf_op jit(solution)/shard_map/all_to_all | solution.py:52
  493.8 2.1 copy.22
  496.0 0.7 convolution_bitcast_fusion.1
  496.7 0.0 collective-permute-done
  496.7 2.3 broadcast_select_fusion.1
  499.0 0.1 fusion.13
  499.1 77.7 %psum.7 = f32[2,32,64]{2,1,0:T(8,128)S(1)} all-reduce(f32[2,32,64]{2,1,0:T(8,128)S(1)} %fusion.13), channel_id=1, replica_groups=mesh['aux'=2,'row'=8,'col'=16] {'aux','row','col'}, use_global_device_ids=true, to_apply=%region_0.1 | all-reduce | flops 4096 | bytes 32768 | tf_op jit(solution)/shard_map/psum | solution.py:69
  576.7 0.6 multiply_bitcast_fusion
  (1 shorter events, 0.0 us)
Async XLA Ops:
  11.1 58.8 %copy-start = (bf16[256,2048]{1,0:T(8,128)(2,1)S(1)}, bf16[256,2048]{1,0:T(8,128)(2,1)}, u32[]{:S(2)}) copy-start(bf16[256,2048]{1,0:T(8,128)(2,1)} %param.5) | copy-start | bytes 3145732
  74.1 270.2 %all-to-all-start.1 = ((bf16[8,256,2048]{2,1,0:T(8,128)(2,1)}), bf16[8,256,2048]{2,1,0:T(8,128)(2,1)}, u32[]{:S(2)}, u32[]{:S(2)}) async-start(bf16[8,256,2048]{2,1,0:T(8,128)(2,1)} %stack.2), calls=%async_computation.1 | async-start | bytes 16777216 | tf_op jit(solution)/shard_map/all_to_all | solution.py:37
  79.1 322.8 %all-gather.2.cloned.1.call-start = ((), (), s32[]{:S(2)}) async-start(), calls=%async_computation.5 | async-start | bytes 9437184 | tf_op jit(solution)/shard_map/all_gather | solution.py:39
  464.2 29.6 %all-to-all-start.4 = ((bf16[32,1,1,16,16,128]{5,3,0,2,1,4:T(8,128)(2,1)}), bf16[32,1,1,16,16,128]{5,3,0,2,1,4:T(8,128)(2,1)}, u32[]{:S(2)}, u32[]{:S(2)}) async-start(bf16[32,1,1,16,16,128]{5,3,0,2,1,4:T(8,128)(2,1)} %copy.21), calls=%async_computation.4 | async-start | bytes 4194304 | tf_op jit(solution)/shard_map/all_to_all | solution.py:52
  468.8 27.9 %collective-permute-start = (bf16[32,256,128]{2,0,1:T(8,128)(2,1)S(1)}, bf16[32,256,128]{2,0,1:T(8,128)(2,1)}, u32[]{:S(2)}, u32[]{:S(2)}) collective-permute-start(bf16[32,256,128]{2,0,1:T(8,128)(2,1)S(1)} %copy_multiply_fusion), channel_id=1, source_target_pairs={{0,128},{128,0},{1,129},{129,1},{2,130},{130,2},{3,131},{131,3},{4... | collective-permute-start | bytes 6291464 | tf_op jit(solution)/shard_map/ppermute | solution.py:13
Sparse Core Ops, SparseCore 0:
  81.8 259.0 all-gather.1
